TPU v7x, 32 devices: a whole 2x2x4 slice. The times are simulated.
32 devices in a mesh: layer: 8 (over z, y), rep: 4 (over x, core).
Axes of the slice: x: 2, y: 2, z: 4, core: 2. Of those that a mesh axis runs over, the one named last changes fastest.
Arguments:
- features: bfloat16 [4096, 128], P('layer'), may hold values from -6 to 6
- weight: bfloat16 [128, 256], replicated, may hold values from -0.5 to 0.5
- out_bias: float32 [256], replicated, may hold values from -3 to 3
- tile_values: bfloat16 [8, 8, 2, 128, 128], P('layer', 'rep'), may hold values from -0.375 to 0.375
- tile_rows: int32 [8, 8, 2], P('layer', 'rep'), may hold values from 0 to 3
- tile_cols: int32 [8, 8, 2], P('layer', 'rep'), may hold values from 0 to 3
- tile_counts: int32 [8, 8, 2], P('layer', 'rep'), may hold values from 0 to 128
- cotangent: bfloat16 [4096, 256], P('layer'), may hold values from -18 to 18
Outputs:
- activation: bfloat16 [4096, 256], P('layer')
- grad_features: bfloat16 [4096, 128], P('layer')
- grad_weight: float32 [128, 256], replicated
- grad_bias: float32 [256], replicated
All inputs are finite; a program needn't handle non-finite values.
Results may differ from a plain program's by a relative error of at most 0.0059.
Values may be sent and summed in bfloat16 or wider, within the bound.
A program may use at most 64 MiB of HBM per device.

v0:
```python
import math

import jax
import jax.numpy as jnp
from jax import lax
from jax.sharding import PartitionSpec as P


def spread(block, axis, holder):
    block = jnp.where(lax.axis_index(axis) == holder, block, jnp.zeros_like(block))
    return lax.psum(block, axis)


def activate(pre_act, grad_in):
    sigmoid_part = jax.nn.sigmoid(pre_act)
    activation = (pre_act * sigmoid_part).astype(jnp.bfloat16)
    grad_pre = (
        grad_in.astype(jnp.float32) * sigmoid_part * (1.0 + pre_act * (1.0 - sigmoid_part))
    ).astype(jnp.bfloat16)
    return (activation, grad_pre)


def local(features, weight, out_bias, tile_values, tile_rows, tile_cols, tile_counts, cotangent):
    rows_dev, hidden = cotangent.shape
    tile_size = tile_values.shape[-1]
    row_tiles = rows_dev // tile_size
    sections = tile_values.shape[1]
    replicas = lax.axis_size("rep")
    share_rows = rows_dev // replicas
    offset = lax.axis_index("rep") * share_rows
    first_section = lax.axis_index("rep") * sections
    projected = jnp.dot(features, weight, preferred_element_type=jnp.float32).astype(jnp.bfloat16)
    lane_ids = jnp.arange(tile_size, dtype=jnp.int32)
    live_tiles = jnp.where(
        lane_ids < tile_counts[0][..., None, None], tile_values[0], jnp.zeros((), jnp.bfloat16)
    )
    tile_range = jnp.arange(row_tiles, dtype=jnp.int32)
    row_hot = (tile_rows[0][..., None] == tile_range).astype(jnp.bfloat16)
    col_hot = (tile_cols[0][..., None] == tile_range).astype(jnp.bfloat16)

    def section_step(section_index, running):
        section_block = spread(projected, "layer", first_section + section_index)
        blocked = section_block.reshape(row_tiles, tile_size, hidden)
        chooser = lax.dynamic_index_in_dim(col_hot, section_index, 0, keepdims=False)
        picked = jnp.einsum(
            "kc,cjf->kjf", chooser, blocked, preferred_element_type=jnp.float32
        ).astype(jnp.bfloat16)
        tile_set = lax.dynamic_index_in_dim(live_tiles, section_index, 0, keepdims=False)
        products = jnp.einsum("kij,kjf->kif", tile_set, picked, preferred_element_type=jnp.float32)
        placer = lax.dynamic_index_in_dim(row_hot, section_index, 0, keepdims=False).astype(
            jnp.float32
        )
        return running + jnp.einsum(
            "kr,kif->rif", placer, products, precision=lax.Precision.HIGHEST
        )

    start_sum = jnp.zeros((row_tiles, tile_size, hidden), jnp.float32)
    aggregate = lax.fori_loop(0, sections, section_step, start_sum).reshape(rows_dev, hidden)
    bias_row = out_bias[None, :]
    share_sum = lax.psum_scatter(aggregate, "rep", scatter_dimension=0, tiled=True)
    own_proj = lax.dynamic_slice_in_dim(projected, offset, share_rows, 0)
    own_grad_in = lax.dynamic_slice_in_dim(cotangent, offset, share_rows, 0)
    pre_act = own_proj.astype(jnp.float32) + share_sum + bias_row
    share_act, share_grad = activate(pre_act, own_grad_in)
    activation, grad_pre = (
        lax.all_gather(share_act, "rep", axis=0, tiled=True),
        lax.all_gather(share_grad, "rep", axis=0, tiled=True),
    )
    grad_tiles = grad_pre.reshape(row_tiles, tile_size, hidden)

    def section_term(pieces):
        tile_set, row_select, col_select = pieces
        picked = jnp.einsum(
            "kr,rif->kif", row_select, grad_tiles, preferred_element_type=jnp.float32
        ).astype(jnp.bfloat16)
        products = jnp.einsum("kij,kif->kjf", tile_set, picked, preferred_element_type=jnp.float32)
        placed = jnp.einsum(
            "kc,kjf->cjf", col_select.astype(jnp.float32), products, precision=lax.Precision.HIGHEST
        )
        return placed.reshape(rows_dev, hidden)

    own_terms = lax.map(section_term, (live_tiles, row_hot, col_hot)).reshape(
        sections * rows_dev, hidden
    )
    own_start = first_section * rows_dev
    own_total = sections * rows_dev
    local_rows = (
        jnp.int32(0) - own_start + jnp.arange(rows_dev * lax.axis_size("layer"), dtype=jnp.int32)
    )
    inside = (local_rows >= 0) & (local_rows < own_total)
    taken_rows = jnp.take(own_terms, jnp.clip(local_rows, 0, own_total - 1), axis=0)
    layer_part = lax.psum_scatter(
        jnp.where(inside[:, None], taken_rows, 0.0), "layer", scatter_dimension=0, tiled=True
    )
    full_terms = lax.psum(layer_part, "rep")
    grad_projected = (grad_pre.astype(jnp.float32) + full_terms).astype(jnp.bfloat16)
    grad_features = lax.dot_general(
        grad_projected, weight, (((1,), (1,)), ((), ())), preferred_element_type=jnp.float32
    ).astype(jnp.bfloat16)
    weight_part = lax.dot_general(
        features, grad_projected, (((0,), (0,)), ((), ())), preferred_element_type=jnp.float32
    )
    bias_part = jnp.sum(grad_pre.astype(jnp.float32), axis=0)
    grad_weight, grad_bias = lax.psum((weight_part, bias_part), "layer")
    node_count = rows_dev * lax.axis_size("layer")
    grad_scale = 1.0 / math.sqrt(node_count)
    return (activation, grad_features, grad_weight * grad_scale, grad_bias * grad_scale)


def solution(mesh):
    in_specs = (
        P("layer", None),
        P(),
        P(),
        P("layer", "rep", None, None, None),
        P("layer", "rep", None),
        P("layer", "rep", None),
        P("layer", "rep", None),
        P("layer", None),
    )
    out_specs = (P("layer", None), P("layer", None), P(), P())
    return jax.shard_map(local, mesh=mesh, in_specs=in_specs, out_specs=out_specs, check_vma=False)
```

profile of v0, /device:TPU:0, one launch (start us, length us, event | category | flops | bytes accessed | tf_op | source)
XLA Modules:
  0.0 432.9 jit_solution(2054064643802026532)
XLA Ops:
  8.0 0.8 iota_compare_fusion
  8.8 0.8 compare_convert_fusion
  9.6 1.0 convolution_convert_fusion
  10.6 0.9 bitcast_select_fusion
  11.6 158.3 %while.25 = (s32[]{:T(128)}, f32[4,128,256]{2,0,1:T(4,128)S(1)}, bf16[2,2,4]{2,1,0:T(2,128)(2,1)S(1)}, bf16[2,2,128,128]{3,2,1,0:T(8,128)(2,1)S(1)}, bf16[2,2,4]...) while((s32[]{:T(128)}, f32[4,128,256]{2,0,1:T(4,128)S(1)}, ...), condition=%wide.region_2.3_spmd.clone, body=%wide.region_0.2_spmd.clone.sunk | while | flops 20971528 | bytes 4261097 | solution.py:58
  11.7 0.7 broadcast_select_fusion.2
  12.4 77.6 %all-reduce.8.cloned.1.call-done = bf16[4,128,256]{2,1,0:T(8,128)(2,1)} async-done(((bf16[4,128,256]{2,1,0:T(8,128)(2,1)}), bf16[4,128,256]{2,1,0:T(8,128)(2,1)}) %all-reduce.8.cloned.1.call-update) | async-done | bytes 262160 | tf_op jit(solution)/shard_map/while/body/eval_jaxpr/psum | solution.py:11
  90.0 1.2 fusion.64
  91.4 1.0 convolution_add_fusion.2
  92.5 0.7 broadcast_select_fusion.2
  93.3 74.2 %all-reduce.8.cloned.1.call-done = bf16[4,128,256]{2,1,0:T(8,128)(2,1)} async-done(((bf16[4,128,256]{2,1,0:T(8,128)(2,1)}), bf16[4,128,256]{2,1,0:T(8,128)(2,1)}) %all-reduce.8.cloned.1.call-update) | async-done | bytes 262160 | tf_op jit(solution)/shard_map/while/body/eval_jaxpr/psum | solution.py:11
  167.4 1.2 fusion.64
  168.9 1.0 convolution_add_fusion.2
  170.0 0.9 copy.15
  171.0 22.7 %reduce-scatter.3.cloned.1.call-done = f32[128,256]{1,0:T(8,128)} async-done(((f32[512,256]{1,0:T(8,128)}), f32[128,256]{1,0:T(8,128)}) %reduce-scatter.3.cloned.1.call-update) | async-done | bytes 131088 | tf_op jit(solution)/shard_map/reduce_scatter | solution.py:60
  193.7 1.0 multiply_convert_fusion
  194.7 5.8 %all_gather.7 = bf16[512,256]{1,0:T(8,128)(2,1)S(1)} all-gather(bf16[128,256]{1,0:T(8,128)(2,1)S(1)} %get-tuple-element.220), channel_id=1, replica_groups=mesh['layer'=8,'rep'=4] {'rep'}, dimensions={0}, use_global_device_ids=true | all-gather | bytes 327680 | tf_op jit(solution)/shard_map/all_gather | solution.py:67
  200.5 3.0 while.24
  201.0 0.8 fusion.58
  202.6 0.8 fusion.58
  203.5 16.2 %gather_fusion = f32[4096,256]{1,0:T(8,128)} fusion(f32[1024,256]{1,0:T(8,128)S(1)} %bitcast.57, s32[4096]{0:T(1024)S(1)} %broadcast_clamp_fusion), kind=kCustom, calls=%fused_computation | custom fusion | bytes 8404992 | tf_op jit(solution)/shard_map/jit(_take)/gather | solution.py:91
  219.7 6.7 %select_select_fusion = f32[4096,256]{1,0:T(8,128)} fusion(f32[4096,256]{1,0:T(8,128)} %gather_fusion, pred[4096]{0:T(1024)(128)(4,1)S(1)} %get-tuple-element.224, pred[4096]{0:T(1024)(128)(4,1)S(1)} %get-tuple-element.225), kind=kLoop, calls=%fused_computation.29 | loop fusion | flops 2097152 | bytes 8396800 | tf_op jit(solution)/shard_map/jit(_where)/select_n | solution.py:93
  226.6 88.0 %reduce-scatter.5.cloned.1.call-done = f32[512,256]{1,0:T(8,128)} async-done(((f32[4096,256]{1,0:T(8,128)}), f32[512,256]{1,0:T(8,128)}) %reduce-scatter.5.cloned.1.call-update) | async-done | bytes 524304 | tf_op jit(solution)/shard_map/reduce_scatter | solution.py:92
  314.7 5.8 %all_gather.6 = bf16[512,256]{1,0:T(8,128)(2,1)S(1)} all-gather(bf16[128,256]{1,0:T(8,128)(2,1)S(1)} %get-tuple-element.221), channel_id=1, replica_groups=mesh['layer'=8,'rep'=4] {'rep'}, dimensions={0}, use_global_device_ids=true | all-gather | bytes 327680 | tf_op jit(solution)/shard_map/all_gather | solution.py:66
  320.4 20.1 %psum.34 = f32[256]{0:T(256)S(1)} all-reduce(f32[256]{0:T(256)S(1)} %convert_reduce_fusion), channel_id=1, replica_groups=mesh['layer'=8,'rep'=4] {'layer'}, use_global_device_ids=true, to_apply=%region_10.11 | all-reduce | flops 256 | bytes 2048 | tf_op jit(solution)/shard_map/psum | solution.py:104
  341.1 8.6 %all-reduce.4.cloned.1.call-done = f32[512,256]{1,0:T(8,128)} async-done(((f32[512,256]{1,0:T(8,128)}), f32[512,256]{1,0:T(8,128)}) %all-reduce.4.cloned.1.call-update) | async-done | bytes 524304 | tf_op jit(solution)/shard_map/psum | solution.py:95
  349.8 2.0 convolution_bitcast_fusion
  351.8 1.9 convolution_convert_fusion.1
  353.7 69.3 %all-reduce.6.cloned.1.call-done = f32[128,256]{0,1:T(8,128)} async-done(((f32[128,256]{0,1:T(8,128)}), f32[128,256]{0,1:T(8,128)}) %all-reduce.6.cloned.1.call-update) | async-done | bytes 131088 | tf_op jit(solution)/shard_map/psum | solution.py:104
  423.0 0.9 broadcast_multiply_fusion
  423.9 0.8 copy.16
  424.6 0.7 copy.67
  (35 shorter events, 2.8 us)
Async XLA Ops:
  8.0 1.6 copy-start
  11.6 182.2 %copy-start.2 = (f32[256]{0:T(256)S(1)}, f32[256]{0:T(256)}, u32[]{:S(2)}) copy-start(f32[256]{0:T(256)} %param.14) | copy-start | bytes 3076
  11.6 78.4 %all-reduce.8.cloned.1.call-start = ((), (), s32[]{:S(2)}) async-start(), calls=%async_computation.6 | async-start | bytes 524288 | tf_op jit(solution)/shard_map/while/body/eval_jaxpr/psum | solution.py:11
  92.5 75.0 %all-reduce.8.cloned.1.call-start = ((), (), s32[]{:S(2)}) async-start(), calls=%async_computation.6 | async-start | bytes 524288 | tf_op jit(solution)/shard_map/while/body/eval_jaxpr/psum | solution.py:11
  169.9 23.8 %reduce-scatter.3.cloned.1.call-start = ((), (), s32[]{:S(2)}) async-start(), calls=%async_computation.2 | async-start | bytes 655360 | tf_op jit(solution)/shard_map/reduce_scatter | solution.py:60
  170.9 143.7 %reduce-scatter.5.cloned.1.call-start = ((), (), s32[]{:S(2)}) async-start(), calls=%async_computation.3 | async-start | bytes 4718592 | tf_op jit(solution)/shard_map/reduce_scatter | solution.py:92
  226.4 125.3 %copy-start.1 = (bf16[128,256]{1,0:T(8,128)(2,1)S(1)}, bf16[128,256]{1,0:T(8,128)(2,1)}, u32[]{:S(2)}) copy-start(bf16[128,256]{1,0:T(8,128)(2,1)} %param.13) | copy-start | bytes 196612
  226.4 123.3 %all-reduce.4.cloned.1.call-start = ((), (), s32[]{:S(2)}) async-start(), calls=%async_computation.4 | async-start | bytes 1048576 | tf_op jit(solution)/shard_map/psum | solution.py:95
  314.6 108.4 %all-reduce.6.cloned.1.call-start = ((), (), s32[]{:S(2)}) async-start(), calls=%async_computation.5 | async-start | bytes 262144 | tf_op jit(solution)/shard_map/psum | solution.py:104
Sparse Core Ops, SparseCore 0:
  16.7 73.2 all-reduce.7
  97.6 69.7 all-reduce.7
Sparse Core Ops, SparseCore 1:
  172.9 20.8 reduce-scatter.2
  226.5 88.0 reduce-scatter.4
  316.8 32.9 all-reduce.3
  353.7 69.2 all-reduce.5
where the time goes:
time: 434 us; the launch traced here: 433 us
  waiting for transfers between devices  340 us (78%)
  blocking collectives  31.7 us (7%)
  local copies, waits for them, and re-layouts  18.8 us (4%)
  between operations  15.8 us (4%)
  other arithmetic  13.3 us (3%)
  matrix products  12.5 us (3%)
    psum x2, waiting for transfers between devices, spread(): return lax.psum(block, axis)  152 us
    reduce_scatter x1, waiting for transfers between devices, local(): lax.psum_scatter(jnp.where(inside[:, None], taken_rows, 0.0), 'layer', sc...  88 us
    psum x1, waiting for transfers between devices, local(): grad_weight, grad_bias = lax.psum((weight_part, bias_part), 'layer')  69.3 us
    reduce_scatter x1, waiting for transfers between devices, local(): lax.psum_scatter(aggregate, 'rep', scatter_dimension=0, tiled=True)  22.7 us
    psum x1, blocking collectives, local(): grad_weight, grad_bias = lax.psum((weight_part, bias_part), 'layer')  20.1 us
    gather x1, local copies, waits for them, and re-layouts, local(): jnp.take(own_terms, jnp.clip(local_rows, 0, own_total - 1), axis=0)  16.2 us
  transfers between devices with their start and end apart: 6, of which 6 were waited for; matrix products, arithmetic and copies ran while one was open for 1% of the time, Pallas kernels for 0%

commit v1 on v0

v1 whole, which is shorter than its diff:
```python
import functools
import math

import jax
import jax.numpy as jnp
from jax import lax
from jax.experimental import pallas as pl
from jax.experimental.pallas import tpu as pltpu
from jax.sharding import PartitionSpec as P

BF = jnp.bfloat16
F32 = jnp.float32
NT = (((1,), (1,)), ((), ()))
NN = (((1,), (0,)), ((), ()))
MESH = pl.DeviceIdType.MESH


def dot(a, b, dims):
    return lax.dot_general(a, b, dims, preferred_element_type=F32)


def kernel(
    L, R, grad_scale,
    feat, w, bias, tv, rows, cols, counts, cot,
    act_o, gf_o, gw_o, gb_o,
    tiles, wt, biasb, cot_t, proj, agg, grad, act_all, gp_all, psend, precv, gwbuf, fin,
    t_send, t_fwd, t_recv, p_send, p_fwd, p_recv, q_send, q_recv,
    a_send, a_recv, g_send, g_recv, w_send, w_recv, f_send, f_recv,
):
    l = lax.axis_index("layer")
    r = lax.axis_index("rep")
    sections, slots, tile = tv.shape[1], tv.shape[2], tv.shape[3]
    hidden = w.shape[1]
    hs = hidden // R
    nt = feat.shape[0] // tile
    meta_at = slots * tile
    metas = tiles.shape[1] - meta_at
    mine = pl.ds(pl.multiple_of(r * hs, hs), hs)

    def remote(src, dst, ssem, rsem, pl_, pr_):
        return pltpu.make_async_remote_copy(
            src_ref=src, dst_ref=dst, send_sem=ssem, recv_sem=rsem,
            device_id={"layer": pl_, "rep": pr_}, device_id_type=MESH,
        )

    def each(n, fn, start=0):
        lax.fori_loop(start, n, lambda i, c: (fn(i), c)[1], 0)

    barrier = pltpu.get_barrier_semaphore()

    def greet_layer(d):
        pl.semaphore_signal(
            barrier, inc=1, device_id={"layer": lax.rem(l + d, L), "rep": r}, device_id_type=MESH)

    def greet_rep(d):
        pl.semaphore_signal(
            barrier, inc=1, device_id={"layer": l, "rep": lax.rem(r + d, R)}, device_id_type=MESH)

    each(L, greet_layer, 1)
    each(R, greet_rep, 1)

    lanes = lax.broadcasted_iota(jnp.int32, (tile, tile), 1)
    row_ids = lax.broadcasted_iota(jnp.int32, (metas, tile), 0)
    for j in range(sections):
        meta = jnp.zeros((metas, tile), F32)
        at = r * sections + j
        for k in range(slots):
            live = jnp.where(lanes < counts[0, j, k], tv[0, j, k].astype(F32), 0.0)
            tiles[at, pl.ds(k * tile, tile), :] = live.astype(BF)
            base = 2 * nt * k
            meta = meta + jnp.where(row_ids == base + rows[0, j, k], 1.0, 0.0)
            meta = meta + jnp.where(row_ids == base + nt + cols[0, j, k], 1.0, 0.0)
        tiles[at, pl.ds(meta_at, metas), :] = meta.astype(BF)

    wt[...] = jnp.transpose(w[...].astype(F32), (1, 0)).astype(BF)
    own = dot(wt[mine, :], feat[...], NT).astype(BF)
    for t in range(nt):
        proj[l, t] = own[:, t * tile:(t + 1) * tile]

    pl.semaphore_wait(barrier, L - 1 + R - 1)

    twin_l = l + 1 - 2 * lax.rem(l, 2)
    twin_r = r + 1 - 2 * lax.rem(r, 2)

    def p_direct(d):
        p = lax.rem(l + 2 * d, L)
        return remote(proj.at[l], proj.at[l], p_send.at[d], p_recv.at[l], p, r)

    def p_forward(d):
        p = lax.rem(l + 2 * d, L)
        return remote(proj.at[p], proj.at[p], p_fwd.at[d], p_recv.at[p], twin_l, r)

    def p_arrival(p):
        return remote(proj.at[p], proj.at[p], p_fwd.at[0], p_recv.at[p], twin_l, r)

    def t_block(q):
        return tiles.at[pl.ds(q * sections, sections)]

    def t_direct(d):
        return remote(t_block(r), t_block(r), t_send.at[d], t_recv.at[r], l, lax.rem(r + 2 * d, R))

    def t_forward(d):
        q = lax.rem(r + 2 * d, R)
        return remote(t_block(q), t_block(q), t_fwd.at[d], t_recv.at[q], l, twin_r)

    def t_arrival(q):
        return remote(t_block(q), t_block(q), t_fwd.at[0], t_recv.at[q], l, twin_r)

    each(R // 2, lambda d: t_direct(d).start(), 1)
    each(L // 2, lambda d: p_direct(L // 2 - d).start(), 1)
    p_forward(0).start()
    t_forward(0).start()

    biasb[...] = jnp.transpose(jnp.broadcast_to(bias[...], (tile, hidden)), (1, 0))
    for t in range(nt):
        part = cot[pl.ds(t * tile, tile), :].astype(F32)
        cot_t[t] = jnp.transpose(part, (1, 0)).astype(BF)

    def relay_tiles(d):
        t_arrival(lax.rem(r + 2 * d, R)).wait_recv()
        t_forward(d).start()

    def relay_proj(d):
        p_arrival(lax.rem(l + 2 * d, L)).wait_recv()
        p_forward(d).start()

    each(R // 2, relay_tiles, 1)
    each(L // 2, relay_proj, 1)
    each(R // 2, lambda d: t_arrival(lax.rem(twin_r + 2 * d, R)).wait_recv())

    agg[...] = jnp.zeros_like(agg)

    def section(s):
        meta = tiles[s, pl.ds(meta_at, metas), :].astype(F32)
        blocks = [proj[s, c].astype(F32) for c in range(nt)]
        sums = [agg[t] for t in range(nt)]
        for k in range(slots):
            base = 2 * nt * k
            picked = sum(
                meta[base + nt + c:base + nt + c + 1, :] * blocks[c] for c in range(nt)
            ).astype(BF)
            product = dot(picked, tiles[s, pl.ds(k * tile, tile), :], NT)
            for t in range(nt):
                sums[t] = sums[t] + meta[base + t:base + t + 1, :] * product
        for t in range(nt):
            agg[t] = sums[t]

    each(L // 2, lambda d: section(lax.rem(l + 2 * d, L)))

    def late_section(d):
        p = lax.rem(twin_l + 2 * d, L)
        p_arrival(p).wait_recv()
        section(p)

    each(L // 2, late_section)

    own_bias = biasb[mine, :]
    for t in range(nt):
        pre = proj[l, t].astype(F32) + agg[t] + own_bias
        sig = jax.nn.sigmoid(pre)
        act_all[t, mine, :] = (pre * sig).astype(BF)
        grad[t] = (cot_t[t, mine, :].astype(F32) * sig * (1.0 + pre * (1.0 - sig))).astype(BF)

    def q_copy(d):
        s = lax.rem(l + d, L)
        return remote(psend.at[s], precv.at[l], q_send.at[d], q_recv.at[l], s, r)

    def products(s, out, at):
        raw = tiles[s, pl.ds(meta_at, metas), :]
        meta = raw.astype(F32)
        blocks = [grad[t].astype(F32) for t in range(nt)]
        for k in range(slots):
            base = 2 * nt * k
            picked = sum(
                meta[base + t:base + t + 1, :] * blocks[t] for t in range(nt)
            ).astype(BF)
            out[at, pl.ds(k * hs, hs), :] = dot(
                picked, tiles[s, pl.ds(k * tile, tile), :], NN).astype(BF)
        out[at, pl.ds(slots * hs, metas), :] = raw

    def send_products(d):
        s = lax.rem(l + d, L)
        products(s, psend, s)
        q_copy(d).start()

    each(L, send_products, 1)

    def rep_copy(buf, at, ssem, rsem, d):
        return remote(buf.at[:, at, :], buf.at[:, at, :], ssem, rsem, l, lax.rem(r + d, R))

    def rep_slice(q):
        return pl.ds(pl.multiple_of(q * hs, hs), hs)

    each(R, lambda d: rep_copy(act_all, mine, a_send.at[d], a_recv.at[r], d).start(), 1)
    products(l, precv, l)

    def a_wait(d):
        q = lax.rem(r + d, R)
        rep_copy(act_all, rep_slice(q), a_send.at[d], a_recv.at[q], d).wait_recv()

    each(R, a_wait, 1)
    for t in range(nt):
        act_o[pl.ds(t * tile, tile), :] = jnp.transpose(
            act_all[t].astype(F32), (1, 0)).astype(BF)

    for t in range(nt):
        agg[t] = grad[t].astype(F32)

    def add_products(p):
        meta = precv[p, pl.ds(slots * hs, metas), :].astype(F32)
        for c in range(nt):
            total = agg[c]
            for k in range(slots):
                at = 2 * nt * k + nt + c
                total = total + meta[at:at + 1, :] * precv[p, pl.ds(k * hs, hs), :].astype(F32)
            agg[c] = total

    add_products(l)

    def take_products(d):
        p = lax.rem(l + d, L)
        remote(precv.at[p], precv.at[p], q_send.at[d], q_recv.at[p], p, r).wait_recv()
        add_products(p)

    each(L, take_products, 1)

    for t in range(nt):
        gp_all[t, mine, :] = agg[t].astype(BF)
    each(R, lambda d: rep_copy(gp_all, mine, g_send.at[d], g_recv.at[r], d).start(), 1)

    gw = jnp.zeros((hs, feat.shape[1]), F32)
    gb = jnp.zeros((metas, tile), F32)
    per = tile // hs
    ones = jnp.ones((metas, tile), BF)
    for t in range(nt):
        gw = gw + dot(gp_all[t, mine, :], feat[pl.ds(t * tile, tile), :], NN)
        gb = gb + dot(ones, jnp.concatenate([grad[t]] * per, axis=0), NT)
    half = lax.broadcasted_iota(jnp.int32, (metas, tile), 1) // hs
    gb = jnp.where(half == lax.rem(r, per), gb, 0.0)
    gwbuf[l, pl.ds(0, hs), :] = gw.astype(BF)
    gwbuf[l, pl.ds(hs, metas), :] = gb.astype(BF)

    def w_copy(d):
        return remote(gwbuf.at[l], gwbuf.at[l], w_send.at[d], w_recv.at[l], lax.rem(l + d, L), r)

    each(L, lambda d: w_copy(d).start(), 1)

    def g_wait(d):
        q = lax.rem(r + d, R)
        rep_copy(gp_all, rep_slice(q), g_send.at[d], g_recv.at[q], d).wait_recv()

    def w_wait(d):
        p = lax.rem(l + d, L)
        remote(gwbuf.at[p], gwbuf.at[p], w_send.at[d], w_recv.at[p], p, r).wait_recv()

    each(L, w_wait, 1)
    fin[r] = (
        lax.fori_loop(0, L, lambda p, c: c + gwbuf[p].astype(F32),
                      jnp.zeros((hs + metas, tile), F32)) * grad_scale
    ).astype(BF)

    def f_copy(q, d):
        return remote(fin.at[q], fin.at[q], f_send.at[d], f_recv.at[q], l, lax.rem(r + d, R))

    each(R, lambda d: f_copy(r, d).start(), 1)

    each(R, g_wait, 1)
    for t in range(nt):
        turned = jnp.transpose(gp_all[t].astype(F32), (1, 0)).astype(BF)
        gf_o[pl.ds(t * tile, tile), :] = dot(turned, w[...], NT).astype(BF)

    each(R, lambda d: f_copy(lax.rem(r + d, R), d).wait_recv(), 1)
    for m in range(R // per):
        group = [fin[per * m + i].astype(F32) for i in range(per)]
        block = jnp.concatenate([g[:hs] for g in group], axis=0)
        gw_o[:, pl.ds(m * tile, tile)] = jnp.transpose(block, (1, 0))
        gb_o[:, pl.ds(m * tile, tile)] = sum(g[hs:hs + 1] for g in group)

    each(R // 2, lambda d: t_direct(d).wait_send(), 1)
    each(R // 2, lambda d: t_forward(d).wait_send())
    each(L // 2, lambda d: p_direct(L // 2 - d).wait_send(), 1)
    each(L // 2, lambda d: p_forward(d).wait_send())
    each(L, lambda d: q_copy(d).wait_send(), 1)
    each(L, lambda d: w_copy(d).wait_send(), 1)

    def rep_sent(d):
        rep_copy(act_all, mine, a_send.at[d], a_recv.at[r], d).wait_send()
        rep_copy(gp_all, mine, g_send.at[d], g_recv.at[r], d).wait_send()
        f_copy(r, d).wait_send()

    each(R, rep_sent, 1)


def local(features, weight, out_bias, tile_values, tile_rows, tile_cols, tile_counts, cotangent):
    L, R = lax.axis_size("layer"), lax.axis_size("rep")
    rows_dev, hidden = cotangent.shape
    f_in = features.shape[1]
    tile = tile_values.shape[-1]
    slots = tile_values.shape[2]
    nt = rows_dev // tile
    hs = hidden // R
    metas = slots * 2 * nt
    vmem = pl.BlockSpec(memory_space=pltpu.VMEM)
    smem = pl.BlockSpec(memory_space=pltpu.SMEM)
    sem = pltpu.SemaphoreType.DMA
    grad_scale = 1.0 / math.sqrt(rows_dev * L)
    act, gf, gw, gb = pl.pallas_call(
        functools.partial(kernel, L, R, grad_scale),
        out_shape=(
            jax.ShapeDtypeStruct((rows_dev, hidden), BF),
            jax.ShapeDtypeStruct((rows_dev, f_in), BF),
            jax.ShapeDtypeStruct((f_in, hidden), F32),
            jax.ShapeDtypeStruct((1, hidden), F32),
        ),
        in_specs=[vmem, vmem, vmem, vmem, smem, smem, smem, vmem],
        out_specs=(vmem, vmem, vmem, vmem),
        scratch_shapes=[
            pltpu.VMEM((L, slots * tile + metas, tile), BF),
            pltpu.VMEM((hidden, f_in), BF),
            pltpu.VMEM((hidden, tile), F32),
            pltpu.VMEM((nt, hidden, tile), BF),
            pltpu.VMEM((L, nt, hs, tile), BF),
            pltpu.VMEM((nt, hs, tile), F32),
            pltpu.VMEM((nt, hs, tile), BF),
            pltpu.VMEM((nt, hidden, tile), BF),
            pltpu.VMEM((nt, hidden, tile), BF),
            pltpu.VMEM((L, slots * hs + metas, tile), BF),
            pltpu.VMEM((L, slots * hs + metas, tile), BF),
            pltpu.VMEM((L, hs + metas, tile), BF),
            pltpu.VMEM((R, hs + metas, tile), BF),
            sem((R,)), sem((R,)), sem((R,)),
            sem((L,)), sem((L,)), sem((L,)),
            sem((L,)), sem((L,)),
            sem((R,)), sem((R,)),
            sem((R,)), sem((R,)),
            sem((L,)), sem((L,)),
            sem((R,)), sem((R,)),
        ],
        compiler_params=pltpu.CompilerParams(
            collective_id=0, has_side_effects=True, vmem_limit_bytes=32 * 1024 * 1024
        ),
        name="graph_layer",
    )(features, weight, out_bias.reshape(1, hidden), tile_values, tile_rows, tile_cols,
      tile_counts, cotangent)
    return act, gf, gw, gb.reshape(hidden)


def solution(mesh):
    in_specs = (
        P("layer", None),
        P(),
        P(),
        P("layer", "rep", None, None, None),
        P("layer", "rep", None),
        P("layer", "rep", None),
        P("layer", "rep", None),
        P("layer", None),
    )
    out_specs = (P("layer", None), P("layer", None), P(), P())
    return jax.shard_map(local, mesh=mesh, in_specs=in_specs, out_specs=out_specs, check_vma=False)
```

time: 434 us -> 42.7 us (0.10)
  waiting for transfers between devices: 340 us -> 0 us
  Pallas kernels: 0 us -> 32.9 us
  blocking collectives: 31.7 us -> 0 us
  between operations: 15.8 us -> 0.66 us
  other arithmetic: 13.3 us -> 0 us
  matrix products: 12.5 us -> 0 us
  local copies, waits for them, and re-layouts: 18.8 us -> 8.88 us
    psum x4 -> x0, waiting for transfers between devices: 230 us -> none  [the longest x2 152 us: spread(): return lax.psum(block, axis)]
    reduce_scatter x2 -> x0, waiting for transfers between devices: 111 us -> none  [the longest x1 88 us: local(): lax.psum_scatter(jnp.where(inside[:, None], taken_rows, 0.0), 'layer', sc...]
    pallas_call x0 -> x1, Pallas kernels: none -> 32.9 us  [local(): pl.pallas_call(functools.partial(kernel, L, R, grad_scale), out_shape=(ja...]
    psum x1 -> x0, blocking collectives: 20.1 us -> none  [local(): grad_weight, grad_bias = lax.psum((weight_part, bias_part), 'layer')]
    gather x1 -> x0, local copies, waits for them, and re-layouts: 16.2 us -> none  [local(): jnp.take(own_terms, jnp.clip(local_rows, 0, own_total - 1), axis=0)]
    dot_general x15 -> x0, matrix products: 12.5 us -> none  [the longest x2 2.49 us: section_step(): jnp.einsum('kc,cjf->kjf', chooser, blocked, preferred_element_type=jnp.fl...]
    all_gather x2 -> x0, blocking collectives: 11.6 us -> none  [the longest x1 5.79 us: local(): lax.all_gather(share_grad, 'rep', axis=0, tiled=True)]
    select_n x5 -> x0, other arithmetic: 9.15 us -> none  [the longest x1 6.74 us: local(): jnp.where(inside[:, None], taken_rows, 0.0)]
  transfers between devices with their start and end apart: 6 -> 0, of which waited for: 6 -> 0; matrix products, arithmetic and copies ran while one was open for 1% -> 0% of each run, Pallas kernels for 0% -> 0%
where the time goes in v1:
time: 42.7 us; the launch traced here: 42.5 us
  Pallas kernels  32.9 us (77%)
  local copies, waits for them, and re-layouts  8.88 us (21%)
  between operations  0.66 us (2%)
    pallas_call x1, Pallas kernels, local(): pl.pallas_call(functools.partial(kernel, L, R, grad_scale), out_shape=(ja...  32.9 us
    unnamed x20, local copies, waits for them, and re-layouts  8.88 us

profile of v1, /device:TPU:0, one launch (start us, length us, event | category | flops | bytes accessed | tf_op | source)
XLA Modules:
  0.0 42.5 jit_solution(15951558967493630966)
XLA Ops:
  0.6 0.0 copy-start.4
  0.6 0.7 %copy-done.4 = f32[256]{0:T(256)S(1)} copy-done((f32[256]{0:T(256)S(1)}, f32[256]{0:T(256)}, u32[]{:S(2)}) %copy-start.4) | copy-done | bytes 1048
  1.3 0.0 copy-start
  1.3 0.9 %copy-done = bf16[512,256]{1,0:T(8,128)(2,1)S(1)} copy-done((bf16[512,256]{1,0:T(8,128)(2,1)S(1)}, bf16[512,256]{1,0:T(8,128)(2,1)}, u32[]{:S(2)}) %copy-start) | copy-done | bytes 262168
  2.3 0.0 copy-start.1
  2.3 0.9 %copy-done.1 = bf16[512,128]{1,0:T(8,128)(2,1)S(1)} copy-done((bf16[512,128]{1,0:T(8,128)(2,1)S(1)}, bf16[512,128]{1,0:T(8,128)(2,1)}, u32[]{:S(2)}) %copy-start.1) | copy-done | bytes 131096
  3.2 0.0 copy-start.2
  3.2 0.9 %copy-done.2 = bf16[1,2,2,128,128]{4,3,2,1,0:T(8,128)(2,1)S(1)} copy-done((bf16[1,2,2,128,128]{4,3,2,1,0:T(8,128)(2,1)S(1)}, bf16[1,2,2,128,128]{4,3,2,1,0:T(8,128)(2,1)}, u32[]{:S(2)}) %copy-start.2) | copy-done | bytes 131096
  4.1 0.0 copy-start.3
  4.1 0.8 %copy-done.3 = bf16[128,256]{1,0:T(8,128)(2,1)S(1)} copy-done((bf16[128,256]{1,0:T(8,128)(2,1)S(1)}, bf16[128,256]{1,0:T(8,128)(2,1)}, u32[]{:S(2)}) %copy-start.3) | copy-done | bytes 65560
  4.9 0.0 copy-start.5
  4.9 0.7 %copy-done.5 = s32[1,2,2]{2,1,0:T(2,128)S(1)} copy-done((s32[1,2,2]{2,1,0:T(2,128)S(1)}, s32[1,2,2]{2,1,0:T(2,128)}, u32[]{:S(2)}) %copy-start.5) | copy-done | bytes 40
  5.6 0.0 copy-start.6
  5.6 0.7 %copy-done.6 = s32[1,2,2]{2,1,0:T(2,128)S(1)} copy-done((s32[1,2,2]{2,1,0:T(2,128)S(1)}, s32[1,2,2]{2,1,0:T(2,128)}, u32[]{:S(2)}) %copy-start.6) | copy-done | bytes 40
  6.3 0.0 copy-start.7
  6.3 0.7 %copy-done.7 = s32[1,2,2]{2,1,0:T(2,128)S(1)} copy-done((s32[1,2,2]{2,1,0:T(2,128)S(1)}, s32[1,2,2]{2,1,0:T(2,128)}, u32[]{:S(2)}) %copy-start.7) | copy-done | bytes 40
  7.0 32.9 %graph_layer.1 = (bf16[512,256]{1,0:T(8,128)(2,1)S(1)}, bf16[512,128]{1,0:T(8,128)(2,1)S(1)}, f32[128,256]{1,0:T(8,128)S(1)}, f32[1,256]{1,0:T(1,128)S(1)}) custom-call(bf16[512,128]{1,0:T(8,128)(2,1)S(1)} %copy-done.1, bf16[128,256]{1,0:T(8,128)(2,1)S(1)} %copy-done.3, f32[1,256]{1,0:T(1,128)S(1)} %bitcast.2, bf16[1,2,2,128,128]{4,3,2,1,0:T(8,128)(2,1)S(1)} %copy-done.2, ...), custom_call_target="tpu_custom_call" | custom-call | tf_op jit(solution)/shard_map/graph_layer/pallas_call | solution.py:307
  39.9 0.7 %copy.16 = bf16[512,256]{1,0:T(8,128)(2,1)} copy(bf16[512,256]{1,0:T(8,128)(2,1)S(1)} %get-tuple-element.16) | data formatting | bytes 524288
  40.6 0.7 %copy.17 = bf16[512,128]{1,0:T(8,128)(2,1)} copy(bf16[512,128]{1,0:T(8,128)(2,1)S(1)} %get-tuple-element.17) | data formatting | bytes 262144
  41.2 0.7 %copy.18 = f32[128,256]{1,0:T(8,128)} copy(f32[128,256]{1,0:T(8,128)S(1)} %get-tuple-element.18) | data formatting | bytes 262144
  41.9 0.6 %copy.19 = f32[256]{0:T(256)} copy(f32[256]{0:T(256)S(1)} %bitcast.3) | data formatting | bytes 2048
Async XLA Ops:
  0.6 0.7 %copy-start.4 = (f32[256]{0:T(256)S(1)}, f32[256]{0:T(256)}, u32[]{:S(2)}) copy-start(f32[256]{0:T(256)} %param.10) | copy-start | bytes 3076
  1.3 0.9 %copy-start = (bf16[512,256]{1,0:T(8,128)(2,1)S(1)}, bf16[512,256]{1,0:T(8,128)(2,1)}, u32[]{:S(2)}) copy-start(bf16[512,256]{1,0:T(8,128)(2,1)} %cot.1) | copy-start | bytes 786436
  2.3 0.9 %copy-start.1 = (bf16[512,128]{1,0:T(8,128)(2,1)S(1)}, bf16[512,128]{1,0:T(8,128)(2,1)}, u32[]{:S(2)}) copy-start(bf16[512,128]{1,0:T(8,128)(2,1)} %feat.1) | copy-start | bytes 393220
  3.2 0.9 %copy-start.2 = (bf16[1,2,2,128,128]{4,3,2,1,0:T(8,128)(2,1)S(1)}, bf16[1,2,2,128,128]{4,3,2,1,0:T(8,128)(2,1)}, u32[]{:S(2)}) copy-start(bf16[1,2,2,128,128]{4,3,2,1,0:T(8,128)(2,1)} %tv.1) | copy-start | bytes 393220
  4.1 0.8 %copy-start.3 = (bf16[128,256]{1,0:T(8,128)(2,1)S(1)}, bf16[128,256]{1,0:T(8,128)(2,1)}, u32[]{:S(2)}) copy-start(bf16[128,256]{1,0:T(8,128)(2,1)} %w.1) | copy-start | bytes 196612
  4.9 0.7 %copy-start.5 = (s32[1,2,2]{2,1,0:T(2,128)S(1)}, s32[1,2,2]{2,1,0:T(2,128)}, u32[]{:S(2)}) copy-start(s32[1,2,2]{2,1,0:T(2,128)} %rows.1) | copy-start | bytes 52
  5.6 0.7 %copy-start.6 = (s32[1,2,2]{2,1,0:T(2,128)S(1)}, s32[1,2,2]{2,1,0:T(2,128)}, u32[]{:S(2)}) copy-start(s32[1,2,2]{2,1,0:T(2,128)} %cols.1) | copy-start | bytes 52
  6.3 0.7 %copy-start.7 = (s32[1,2,2]{2,1,0:T(2,128)S(1)}, s32[1,2,2]{2,1,0:T(2,128)}, u32[]{:S(2)}) copy-start(s32[1,2,2]{2,1,0:T(2,128)} %counts.1) | copy-start | bytes 52

commit v2 on v1

--- a/solution.py
+++ b/solution.py
@@ -21,8 +21,9 @@
 
 def kernel(
     L, R, grad_scale,
-    feat, w, bias, tv, rows, cols, counts, cot,
+    feat_h, w_h, bias_h, tv_h, rows_h, cols_h, counts_h, cot_h,
     act_o, gf_o, gw_o, gb_o,
+    feat, w, bias, tv, rows, cols, counts, cot, in_sem,
     tiles, wt, biasb, cot_t, proj, agg, grad, act_all, gp_all, psend, precv, gwbuf, fin,
     t_send, t_fwd, t_recv, p_send, p_fwd, p_recv, q_send, q_recv,
     a_send, a_recv, g_send, g_recv, w_send, w_recv, f_send, f_recv,
@@ -47,6 +48,14 @@
         lax.fori_loop(start, n, lambda i, c: (fn(i), c)[1], 0)
 
     barrier = pltpu.get_barrier_semaphore()
+    loads = [
+        pltpu.make_async_copy(src, dst, in_sem.at[i])
+        for i, (src, dst) in enumerate((
+            (counts_h, counts), (rows_h, rows), (cols_h, cols), (tv_h, tv),
+            (w_h, w), (feat_h, feat), (bias_h, bias), (cot_h, cot)))
+    ]
+    for load in loads:
+        load.start()
 
     def greet_layer(d):
         pl.semaphore_signal(
@@ -59,6 +68,8 @@
     each(L, greet_layer, 1)
     each(R, greet_rep, 1)
 
+    for load in loads[:4]:
+        load.wait()
     lanes = lax.broadcasted_iota(jnp.int32, (tile, tile), 1)
     row_ids = lax.broadcasted_iota(jnp.int32, (metas, tile), 0)
     for j in range(sections):
@@ -72,6 +83,8 @@
             meta = meta + jnp.where(row_ids == base + nt + cols[0, j, k], 1.0, 0.0)
         tiles[at, pl.ds(meta_at, metas), :] = meta.astype(BF)
 
+    for load in loads[4:6]:
+        load.wait()
     wt[...] = jnp.transpose(w[...].astype(F32), (1, 0)).astype(BF)
     own = dot(wt[mine, :], feat[...], NT).astype(BF)
     for t in range(nt):
@@ -111,6 +124,8 @@
     p_forward(0).start()
     t_forward(0).start()
 
+    for load in loads[6:]:
+        load.wait()
     biasb[...] = jnp.transpose(jnp.broadcast_to(bias[...], (tile, hidden)), (1, 0))
     for t in range(nt):
         part = cot[pl.ds(t * tile, tile), :].astype(F32)
@@ -291,6 +306,27 @@
     each(R, rep_sent, 1)
 
 
+def write_kernel(*refs):
+    n = (len(refs) - 1) // 2
+    copies = [pltpu.make_async_copy(refs[i], refs[n + i], refs[-1].at[i]) for i in range(n)]
+    for copy in copies:
+        copy.start()
+    for copy in copies:
+        copy.wait()
+
+
+def write_out(*arrays):
+    n = len(arrays)
+    return pl.pallas_call(
+        write_kernel,
+        out_shape=tuple(jax.ShapeDtypeStruct(a.shape, a.dtype) for a in arrays),
+        in_specs=[pl.BlockSpec(memory_space=pltpu.VMEM)] * n,
+        out_specs=(pl.BlockSpec(memory_space=pltpu.HBM),) * n,
+        scratch_shapes=[pltpu.SemaphoreType.DMA((n,))],
+        name="write_out",
+    )(*[pltpu.with_memory_space_constraint(a, pltpu.VMEM) for a in arrays])
+
+
 def local(features, weight, out_bias, tile_values, tile_rows, tile_cols, tile_counts, cotangent):
     L, R = lax.axis_size("layer"), lax.axis_size("rep")
     rows_dev, hidden = cotangent.shape
@@ -301,7 +337,7 @@
     hs = hidden // R
     metas = slots * 2 * nt
     vmem = pl.BlockSpec(memory_space=pltpu.VMEM)
-    smem = pl.BlockSpec(memory_space=pltpu.SMEM)
+    hbm = pl.BlockSpec(memory_space=pltpu.HBM)
     sem = pltpu.SemaphoreType.DMA
     grad_scale = 1.0 / math.sqrt(rows_dev * L)
     act, gf, gw, gb = pl.pallas_call(
@@ -312,9 +348,18 @@
             jax.ShapeDtypeStruct((f_in, hidden), F32),
             jax.ShapeDtypeStruct((1, hidden), F32),
         ),
-        in_specs=[vmem, vmem, vmem, vmem, smem, smem, smem, vmem],
+        in_specs=[hbm] * 8,
         out_specs=(vmem, vmem, vmem, vmem),
         scratch_shapes=[
+            pltpu.VMEM(features.shape, BF),
+            pltpu.VMEM(weight.shape, BF),
+            pltpu.VMEM((1, hidden), F32),
+            pltpu.VMEM(tile_values.shape, BF),
+            pltpu.SMEM(tile_rows.shape, jnp.int32),
+            pltpu.SMEM(tile_rows.shape, jnp.int32),
+            pltpu.SMEM(tile_rows.shape, jnp.int32),
+            pltpu.VMEM(cotangent.shape, BF),
+            sem((8,)),
             pltpu.VMEM((L, slots * tile + metas, tile), BF),
             pltpu.VMEM((hidden, f_in), BF),
             pltpu.VMEM((hidden, tile), F32),
@@ -340,9 +385,10 @@
             collective_id=0, has_side_effects=True, vmem_limit_bytes=32 * 1024 * 1024
         ),
         name="graph_layer",
-    )(features, weight, out_bias.reshape(1, hidden), tile_values, tile_rows, tile_cols,
-      tile_counts, cotangent)
-    return act, gf, gw, gb.reshape(hidden)
+    )(*[pltpu.with_memory_space_constraint(x, pltpu.HBM) for x in (
+        features, weight, out_bias.reshape(1, hidden), tile_values, tile_rows, tile_cols,
+        tile_counts, cotangent)])
+    return write_out(act, gf, gw, gb.reshape(hidden))
 
 
 def solution(mesh):

time: 42.7 us -> 34.3 us (0.80)
  local copies, waits for them, and re-layouts: 8.88 us -> 0 us
  Pallas kernels: 32.9 us -> 33.5 us
    unnamed x20 -> x0, local copies, waits for them, and re-layouts: 8.88 us -> none
    pallas_call x0 -> x1, Pallas kernels: none -> 0.82 us  [write_out(): pl.pallas_call(write_kernel, out_shape=tuple((jax.ShapeDtypeStruct(a.shap...]
where the time goes in v2:
time: 34.3 us; the launch traced here: 34.2 us
  Pallas kernels  33.5 us (98%)
  between operations  0.64 us (2%)
    pallas_call x1, Pallas kernels, local(): pl.pallas_call(functools.partial(kernel, L, R, grad_scale), out_shape=(ja...  32.7 us
    pallas_call x1, Pallas kernels, write_out(): pl.pallas_call(write_kernel, out_shape=tuple((jax.ShapeDtypeStruct(a.shap...  0.82 us

profile of v2, /device:TPU:0, one launch (start us, length us, event | category | flops | bytes accessed | tf_op | source)
XLA Modules:
  0.0 34.2 jit_solution(3298019230822776828)
XLA Ops:
  0.6 32.7 %graph_layer.1 = (bf16[512,256]{1,0:T(8,128)(2,1)S(1)}, bf16[512,128]{1,0:T(8,128)(2,1)S(1)}, f32[128,256]{1,0:T(8,128)S(1)}, f32[1,256]{1,0:T(1,128)S(1)}) custom-call(bf16[512,128]{1,0:T(8,128)(2,1)} %feat_h.1, bf16[128,256]{1,0:T(8,128)(2,1)} %w_h.1, f32[1,256]{1,0:T(1,128)} %bitcast.3, bf16[1,2,2,128,128]{4,3,2,1,0:T(8,128)(2,1)} %tv_h.1, ...), custom_call_target="tpu_custom_call" | custom-call | tf_op jit(solution)/shard_map/graph_layer/pallas_call | solution.py:343
  33.4 0.8 %write_out.1 = (bf16[512,256]{1,0:T(8,128)(2,1)}, bf16[512,128]{1,0:T(8,128)(2,1)}, f32[128,256]{1,0:T(8,128)}, f32[256]{0:T(256)}) custom-call(bf16[512,256]{1,0:T(8,128)(2,1)S(1)} %get-tuple-element.8.refs_0_, bf16[512,128]{1,0:T(8,128)(2,1)S(1)} %get-tuple-element.9.refs_1_, f32[128,256]{1,0:T(8,128)S(1)} %get-tuple-element.10.refs_2_, f32[256]{0:T(256)S(1)} %bitcast.2), custom_call_target="tpu_custom_call" | custom-call | tf_op jit(solution)/shard_map/write_out/pallas_call | solution.py:320

commit v3 on v2

--- a/solution.py
+++ b/solution.py
@@ -198,7 +198,7 @@
         products(s, psend, s)
         q_copy(d).start()
 
-    each(L, send_products, 1)
+    each(L, lambda d: send_products(L - d), 1)
 
     def rep_copy(buf, at, ssem, rsem, d):
         return remote(buf.at[:, at, :], buf.at[:, at, :], ssem, rsem, l, lax.rem(r + d, R))
@@ -230,6 +230,14 @@
                 total = total + meta[at:at + 1, :] * precv[p, pl.ds(k * hs, hs), :].astype(F32)
             agg[c] = total
 
+    gb = jnp.zeros((metas, tile), F32)
+    per = tile // hs
+    ones = jnp.ones((metas, tile), BF)
+    for t in range(nt):
+        gb = gb + dot(ones, jnp.concatenate([grad[t]] * per, axis=0), NT)
+    half = lax.broadcasted_iota(jnp.int32, (metas, tile), 1) // hs
+    gwbuf[l, pl.ds(hs, metas), :] = jnp.where(half == lax.rem(r, per), gb, 0.0).astype(BF)
+
     add_products(l)
 
     def take_products(d):
@@ -243,17 +251,8 @@
         gp_all[t, mine, :] = agg[t].astype(BF)
     each(R, lambda d: rep_copy(gp_all, mine, g_send.at[d], g_recv.at[r], d).start(), 1)
 
-    gw = jnp.zeros((hs, feat.shape[1]), F32)
-    gb = jnp.zeros((metas, tile), F32)
-    per = tile // hs
-    ones = jnp.ones((metas, tile), BF)
-    for t in range(nt):
-        gw = gw + dot(gp_all[t, mine, :], feat[pl.ds(t * tile, tile), :], NN)
-        gb = gb + dot(ones, jnp.concatenate([grad[t]] * per, axis=0), NT)
-    half = lax.broadcasted_iota(jnp.int32, (metas, tile), 1) // hs
-    gb = jnp.where(half == lax.rem(r, per), gb, 0.0)
+    gw = dot(jnp.concatenate([agg[t].astype(BF) for t in range(nt)], axis=1), feat[...], NN)
     gwbuf[l, pl.ds(0, hs), :] = gw.astype(BF)
-    gwbuf[l, pl.ds(hs, metas), :] = gb.astype(BF)
 
     def w_copy(d):
         return remote(gwbuf.at[l], gwbuf.at[l], w_send.at[d], w_recv.at[l], lax.rem(l + d, L), r)

time: 34.3 us -> 33.7 us (0.983)
  Pallas kernels: 33.5 us -> 32.9 us
    pallas_call x1, Pallas kernels: 32.7 us -> 32.1 us  [local(): pl.pallas_call(functools.partial(kernel, L, R, grad_scale), out_shape=(ja...]
where the time goes in v3:
time: 33.7 us; the launch traced here: 33.6 us
  Pallas kernels  32.9 us (98%)
  between operations  0.64 us (2%)
    pallas_call x1, Pallas kernels, local(): pl.pallas_call(functools.partial(kernel, L, R, grad_scale), out_shape=(ja...  32.1 us
    pallas_call x1, Pallas kernels, write_out(): pl.pallas_call(write_kernel, out_shape=tuple((jax.ShapeDtypeStruct(a.shap...  0.82 us

profile of v3, /device:TPU:0, one launch (start us, length us, event | category | flops | bytes accessed | tf_op | source)
XLA Modules:
  0.0 33.6 jit_solution(1472841074933228029)
XLA Ops:
  0.6 32.1 %graph_layer.1 = (bf16[512,256]{1,0:T(8,128)(2,1)S(1)}, bf16[512,128]{1,0:T(8,128)(2,1)S(1)}, f32[128,256]{1,0:T(8,128)S(1)}, f32[1,256]{1,0:T(1,128)S(1)}) custom-call(bf16[512,128]{1,0:T(8,128)(2,1)} %feat_h.1, bf16[128,256]{1,0:T(8,128)(2,1)} %w_h.1, f32[1,256]{1,0:T(1,128)} %bitcast.3, bf16[1,2,2,128,128]{4,3,2,1,0:T(8,128)(2,1)} %tv_h.1, ...), custom_call_target="tpu_custom_call" | custom-call | tf_op jit(solution)/shard_map/graph_layer/pallas_call | solution.py:342
  32.7 0.8 %write_out.1 = (bf16[512,256]{1,0:T(8,128)(2,1)}, bf16[512,128]{1,0:T(8,128)(2,1)}, f32[128,256]{1,0:T(8,128)}, f32[256]{0:T(256)}) custom-call(bf16[512,256]{1,0:T(8,128)(2,1)S(1)} %get-tuple-element.8.refs_0_, bf16[512,128]{1,0:T(8,128)(2,1)S(1)} %get-tuple-element.9.refs_1_, f32[128,256]{1,0:T(8,128)S(1)} %get-tuple-element.10.refs_2_, f32[256]{0:T(256)S(1)} %bitcast.2), custom_call_target="tpu_custom_call" | custom-call | tf_op jit(solution)/shard_map/write_out/pallas_call | solution.py:319

commit v4 on v3

--- a/solution.py
+++ b/solution.py
@@ -176,6 +176,9 @@
         act_all[t, mine, :] = (pre * sig).astype(BF)
         grad[t] = (cot_t[t, mine, :].astype(F32) * sig * (1.0 + pre * (1.0 - sig))).astype(BF)
 
+    def rep_copy(buf, at, ssem, rsem, d):
+        return remote(buf.at[:, at, :], buf.at[:, at, :], ssem, rsem, l, lax.rem(r + d, R))
+
     def q_copy(d):
         s = lax.rem(l + d, L)
         return remote(psend.at[s], precv.at[l], q_send.at[d], q_recv.at[l], s, r)
@@ -198,15 +201,13 @@
         products(s, psend, s)
         q_copy(d).start()
 
-    each(L, lambda d: send_products(L - d), 1)
-
-    def rep_copy(buf, at, ssem, rsem, d):
-        return remote(buf.at[:, at, :], buf.at[:, at, :], ssem, rsem, l, lax.rem(r + d, R))
+    each(L // 2, lambda d: send_products(L - d), 1)
+    each(R, lambda d: rep_copy(act_all, mine, a_send.at[d], a_recv.at[r], d).start(), 1)
+    each(L, lambda d: send_products(L - d), L // 2)
 
     def rep_slice(q):
         return pl.ds(pl.multiple_of(q * hs, hs), hs)
 
-    each(R, lambda d: rep_copy(act_all, mine, a_send.at[d], a_recv.at[r], d).start(), 1)
     products(l, precv, l)
 
     def a_wait(d):

time: 33.7 us -> 33.7 us (level)
  no operation moved by 1% of the time
where the time goes in v4:
time: 33.7 us; the launch traced here: 33.6 us
  Pallas kernels  32.9 us (98%)
  between operations  0.64 us (2%)
    pallas_call x1, Pallas kernels, local(): pl.pallas_call(functools.partial(kernel, L, R, grad_scale), out_shape=(ja...  32.1 us
    pallas_call x1, Pallas kernels, write_out(): pl.pallas_call(write_kernel, out_shape=tuple((jax.ShapeDtypeStruct(a.shap...  0.82 us

profile of v4, /device:TPU:0, one launch (start us, length us, event | category | flops | bytes accessed | tf_op | source)
XLA Modules:
  0.0 33.6 jit_solution(12584742314171923770)
XLA Ops:
  0.6 32.1 %graph_layer.1 = (bf16[512,256]{1,0:T(8,128)(2,1)S(1)}, bf16[512,128]{1,0:T(8,128)(2,1)S(1)}, f32[128,256]{1,0:T(8,128)S(1)}, f32[1,256]{1,0:T(1,128)S(1)}) custom-call(bf16[512,128]{1,0:T(8,128)(2,1)} %feat_h.1, bf16[128,256]{1,0:T(8,128)(2,1)} %w_h.1, f32[1,256]{1,0:T(1,128)} %bitcast.3, bf16[1,2,2,128,128]{4,3,2,1,0:T(8,128)(2,1)} %tv_h.1, ...), custom_call_target="tpu_custom_call" | custom-call | tf_op jit(solution)/shard_map/graph_layer/pallas_call | solution.py:343
  32.8 0.8 %write_out.1 = (bf16[512,256]{1,0:T(8,128)(2,1)}, bf16[512,128]{1,0:T(8,128)(2,1)}, f32[128,256]{1,0:T(8,128)}, f32[256]{0:T(256)}) custom-call(bf16[512,256]{1,0:T(8,128)(2,1)S(1)} %get-tuple-element.8.refs_0_, bf16[512,128]{1,0:T(8,128)(2,1)S(1)} %get-tuple-element.9.refs_1_, f32[128,256]{1,0:T(8,128)S(1)} %get-tuple-element.10.refs_2_, f32[256]{0:T(256)S(1)} %bitcast.2), custom_call_target="tpu_custom_call" | custom-call | tf_op jit(solution)/shard_map/write_out/pallas_call | solution.py:320
